TPU v7x, 32 devices: a whole 2x2x4 slice. The times are simulated.
32 devices in a mesh: mem: 8 (over z, y), tile: 4 (over x, core).
Axes of the slice: x: 2, y: 2, z: 4, core: 2. Of those that a mesh axis runs over, the one named last changes fastest.
Arguments:
- initial_realization_fields: float32 [128, 3, 4, 32, 128], P('mem', None, None, 'tile'), may hold values from -6 to 6, as said below
- measurement_location_offset: int32 [1024], replicated, may hold values from 0 to 32767
- observed: float32 [1024], P('tile'), may hold values from -6 to 6
- obs_var: float32 [1024], P('tile'), may hold values from 0.25 to 4
- obs_noise: float32 [1024, 128], P('tile', 'mem'), may hold values from -6 to 6
Outputs:
- analysis: float32 [128, 3, 4, 32, 128], P('mem', None, None, 'tile')
Inputs may be any that keep to these rules, and one draw needn't show every extreme that they name: `initial_realization_fields`: field 0 of each member is the log-conductivity, field 1 the head, field 2 the salinity.
All inputs are finite; a program needn't handle non-finite values.
Results may differ from a plain program's by a relative error of at most 0.000076.
Values sent between devices are 32-bit elements; how exact they have to be, the bound alone decides.
A program may use at most 64 MiB of HBM per device.

v0:
```python
import math

import jax
import jax.numpy as jnp
from jax import lax
from jax.sharding import PartitionSpec as P

alpha_mda = 4.0
buoyancy = 0.5
head_rate = 0.02
salt_diffusion = 0.01
salt_advection = 0.01


def with_halo(cells, sides, width):
    for axis, dim in sides:
        count = lax.axis_size(axis)
        ends = count - 1
        head = lax.slice_in_dim(cells, 0, width, axis=dim)
        tail = lax.slice_in_dim(cells, cells.shape[dim] - width, cells.shape[dim], axis=dim)
        cells = jnp.concatenate(
            [
                lax.ppermute(tail, axis, [(i, (i + 1) % count) for i in range(ends)]),
                cells,
                lax.ppermute(head, axis, [((i + 1) % count, i) for i in range(ends)]),
            ],
            axis=dim,
        )
    return cells


def neighbours(padded):
    return [
        padded[:, :-2, 1:-1, 1:-1],
        padded[:, 2:, 1:-1, 1:-1],
        padded[:, 1:-1, :-2, 1:-1],
        padded[:, 1:-1, 2:, 1:-1],
        padded[:, 1:-1, 1:-1, :-2],
        padded[:, 1:-1, 1:-1, 2:],
    ]


def transport(cond_pad, head_pad, salt_pad):
    conduct = cond_pad[:, 1:-1, 1:-1, 1:-1]
    head_now = head_pad[:, 1:-1, 1:-1, 1:-1]
    salt_now = salt_pad[:, 1:-1, 1:-1, 1:-1]
    head_sum = jnp.zeros_like(head_now)
    salt_sum = jnp.zeros_like(salt_now)
    directions = (-1.0, 1.0, 0.0, 0.0, 0.0, 0.0)
    for buoyant, cond_nb, head_nb, salt_nb in zip(
        directions, neighbours(cond_pad), neighbours(head_pad), neighbours(salt_pad)
    ):
        face_cond = 2.0 * conduct * cond_nb / (conduct + cond_nb)
        face_flux = face_cond * (
            head_nb - head_now + buoyant * buoyancy * 0.5 * (salt_now + salt_nb)
        )
        head_sum = head_sum + face_flux
        salt_sum = (
            salt_sum
            + salt_diffusion * face_cond * (salt_nb - salt_now)
            + salt_advection * face_flux * 0.5 * (salt_now + salt_nb)
        )
    return (head_now + head_rate * head_sum, salt_now + salt_sum)


def products(all_data, all_innov, part_scale, realization_stack):
    anomaly = (all_data - jnp.mean(all_data, axis=0, keepdims=True)) / (
        part_scale[None, :] * math.sqrt(realization_stack - 1)
    )
    gram_part = jnp.dot(
        anomaly, anomaly.T, precision=lax.Precision.HIGHEST, preferred_element_type=jnp.float32
    )
    cross_part = jnp.dot(
        anomaly, all_innov.T, precision=lax.Precision.HIGHEST, preferred_element_type=jnp.float32
    )
    return (gram_part, cross_part)


def local(initial_realization_fields, measurement_location_offset, observed, obs_var, obs_noise):
    realization_total, fields, layers, width_x, width_y = initial_realization_fields.shape
    tile_rank = lax.axis_index("tile")
    tile_count = lax.axis_size("tile")
    rimmed = with_halo(initial_realization_fields, (("tile", 3),), 1)
    padded = jnp.pad(rimmed, ((0, 0), (0, 0), (1, 1), (0, 0), (1, 1)))
    grid_pad = padded.shape[2:]
    layer_pos = lax.broadcasted_iota(jnp.int32, grid_pad, 0)
    row_pos = lax.broadcasted_iota(jnp.int32, grid_pad, 1)
    col_pos = lax.broadcasted_iota(jnp.int32, grid_pad, 2)
    inside = (layer_pos >= 1) & (layer_pos <= layers) & (col_pos >= 1) & (col_pos <= width_y)
    inside = (
        inside
        & ((row_pos >= 1) | (tile_rank > 0))
        & ((row_pos <= width_x) | (tile_rank < tile_count - 1))
    )
    cond_pad = jnp.where(inside[None], jnp.exp(padded[:, 0]), 0.0)
    stepped_hydraulic_level, stepped_solute_concentration = transport(
        cond_pad, padded[:, 1], padded[:, 2]
    )
    trial_realization = jnp.stack(
        [initial_realization_fields[:, 0], stepped_hydraulic_level, stepped_solute_concentration],
        axis=1,
    )
    plane_size = width_x * tile_count * width_y
    per_field = layers * plane_size
    field_id = measurement_location_offset // per_field
    remainder = measurement_location_offset % per_field
    layer_id = remainder // plane_size
    plane_pos = remainder % plane_size
    local_row = plane_pos // width_y - tile_rank * width_x
    col_id = plane_pos % width_y
    is_owned = (local_row >= 0) & (local_row < width_x)
    local_index = (
        (field_id * layers + layer_id) * width_x + jnp.clip(local_row, 0, width_x - 1)
    ) * width_y + col_id
    raveled_measured_vector = trial_realization[:, 1:3].reshape(realization_total, -1)
    values = jnp.take(raveled_measured_vector, local_index, axis=1)
    partial_data = jnp.where(is_owned[None, :], values, 0.0)
    own_data = lax.psum_scatter(partial_data, "tile", scatter_dimension=1, tiled=True)
    obs_scale = jnp.sqrt(alpha_mda * obs_var)
    innovation = (observed[None, :] - own_data) / obs_scale[None, :] + obs_noise.T
    realization_stack = realization_total * lax.axis_size("mem")
    mem_rank = lax.axis_index("mem")
    all_data, all_innov = (
        lax.all_gather(own_data, "mem", axis=0, tiled=True),
        lax.all_gather(innovation, "mem", axis=0, tiled=True),
    )
    gram_part, cross_part = products(all_data, all_innov, obs_scale, realization_stack)
    gram_sum, cross_sum = lax.psum((gram_part, cross_part), "tile")
    identity = jnp.eye(realization_stack, dtype=jnp.float32)
    lower_factor = jnp.linalg.cholesky(identity + gram_sum)
    half_solve = lax.linalg.triangular_solve(lower_factor, cross_sum, left_side=True, lower=True)
    weights = lax.linalg.triangular_solve(
        lower_factor, half_solve, left_side=True, lower=True, transpose_a=True
    )
    scaled = weights / math.sqrt(realization_stack - 1)
    blend_weight = identity + scaled - jnp.mean(scaled, axis=0, keepdims=True)
    mesh_volumes = fields * layers * width_x * width_y
    raveled_trial_vector = trial_realization.reshape(realization_total, mesh_volumes)
    own_columns = lax.dynamic_slice_in_dim(
        blend_weight, mem_rank * realization_total, realization_total, 1
    )
    result = jnp.dot(
        own_columns.T,
        lax.all_gather(raveled_trial_vector, "mem", axis=0, tiled=True),
        precision=lax.Precision.HIGHEST,
        preferred_element_type=jnp.float32,
    )
    return result.reshape(initial_realization_fields.shape)


def solution(mesh):
    in_specs = (P("mem", None, None, "tile", None), P(), P("tile"), P("tile"), P("tile", "mem"))
    out_specs = P("mem", None, None, "tile", None)
    return jax.shard_map(local, mesh=mesh, in_specs=in_specs, out_specs=out_specs, check_vma=False)
```

profile of v0, /device:TPU:0, one launch (start us, length us, event | category | flops | bytes accessed | tf_op | source)
XLA Modules:
  0.0 233.2 jit_solution(15137658629228714168)
XLA Ops:
  7.4 1.6 fusion.50
  9.0 2.4 %collective-permute-start = (f32[16,3,4,1,128]{4,0,3,2,1:T(8,128)S(1)}, f32[16,3,4,1,128]{4,0,3,2,1:T(8,128)S(1)}, u32[]{:S(2)}, u32[]{:S(2)}) collective-permute-start(f32[16,3,4,1,128]{4,0,3,2,1:T(8,128)S(1)} %copy.34), channel_id=1, source_target_pairs={{0,1},{1,2},{2,3},{4,5},{5,6},{6,7},{8,9},{9,10},{10,11},{12,13},{... | collective-permute-start | bytes 294920 | tf_op jit(solution)/shard_map/ppermute | solution.py:23
  11.4 1.3 collective-permute-start.1
  12.8 0.7 compare_and_fusion
  13.7 3.0 %collective-permute-done.1 = f32[16,3,4,1,128]{4,0,3,2,1:T(8,128)S(1)} collective-permute-done((f32[16,3,4,1,128]{4,0,3,2,1:T(8,128)S(1)}, f32[16,3,4,1,128]{4,0,3,2,1:T(8,128)S(1)}, u32[]{:S(2)}, u32[]{:S(2)}) %collective-permute-start.1) | collective-permute-done | bytes 98336 | tf_op jit(solution)/shard_map/ppermute | solution.py:25
  16.8 3.2 %select_maximum_fusion = f32[16,3,6,10,130]{4,3,2,0,1:T(8,128)S(1)} fusion(f32[16,3,4,1,128]{4,3,2,0,1:T(1,128)S(1)} %copy.28, f32[16,3,4,1,128]{4,3,2,0,1:T(1,128)S(1)} %copy.26, f32[16,3,4,8,128]{4,3,2,1,0:T(8,128)} %param.5), kind=kLoop, calls=%fused_computation.5 | loop fusion | flops 5616000 | bytes 2480640 | tf_op jit(solution)/shard_map/concatenate | solution.py:21
  20.0 0.4 slice_bitcast_fusion
  20.4 0.2 fusion.4
  20.6 1.3 add_bitcast_fusion.1
  21.9 1.1 add_bitcast_fusion
  23.1 2.6 %copy.29 = f32[16,2,4,8,128]{0,4,3,2,1:T(8,128)} copy(f32[16,2,4,8,128]{4,3,2,1,0:T(8,128)S(1)} %pad_maximum_fusion.1) | data formatting | bytes 1048576 | tf_op jit(solution)/shard_map/stack | solution.py:99
  25.7 5.0 %gather_fusion = f32[1024,16]{1,0:T(8,128)S(1)} fusion(f32[16,8192]{0,1:T(8,128)} %bitcast.43, s32[1024]{0:T(1024)S(1)} %broadcast_clamp_fusion), kind=kCustom, calls=%fused_computation | custom fusion | bytes 135168 | tf_op jit(solution)/shard_map/jit(_take)/gather | solution.py:116
  30.8 0.7 select_bitcast_fusion
  31.6 22.8 %reduce-scatter.2.cloned.1.call-done = f32[16,256]{1,0:T(8,128)} async-done(((f32[16,1024]{1,0:T(8,128)}), f32[16,256]{1,0:T(8,128)}) %reduce-scatter.2.cloned.1.call-update) | async-done | bytes 16400 | tf_op jit(solution)/shard_map/reduce_scatter | solution.py:118
  54.4 30.8 %all_gather.9 = f32[128,256]{1,0:T(8,128)S(1)} all-gather(f32[16,256]{1,0:T(8,128)} %reduce-scatter.2.cloned.1.call-done), channel_id=1, replica_groups=mesh['mem'=8,'tile'=4] {'mem'}, dimensions={0}, use_global_device_ids=true | all-gather | bytes 147456 | tf_op jit(solution)/shard_map/all_gather | solution.py:124
  85.3 0.7 bitcast_add_fusion.1
  86.0 30.5 %all_gather.10 = f32[128,256]{1,0:T(8,128)S(1)} all-gather(f32[16,256]{1,0:T(8,128)S(1)} %bitcast_add_fusion.1), channel_id=1, replica_groups=mesh['mem'=8,'tile'=4] {'mem'}, dimensions={0}, use_global_device_ids=true | all-gather | bytes 147456 | tf_op jit(solution)/shard_map/all_gather | solution.py:125
  116.5 0.9 fusion.27
  117.4 0.9 fusion.26
  118.4 0.2 all-gather.2.cloned.1.call-start
  118.7 1.3 copy.41
  120.1 30.3 %all-reduce.4.cloned.1.call-done = (f32[128,128]{1,0:T(8,128)}, f32[128,128]{1,0:T(8,128)}) async-done(((f32[128,128]{1,0:T(8,128)}, f32[128,128]{1,0:T(8,128)}), (f32[128,128]{1,0:T(8,128)}, f32[128,128]{1,0:T(8,128)})) %all-reduce.4.cloned.1.call-update) | async-done | bytes 131088 | tf_op jit(solution)/shard_map/psum | solution.py:128
  150.3 0.9 fusion.29
  151.3 0.9 fusion.24
  152.2 11.7 %cholesky.14 = f32[128,128]{1,0:T(8,128)S(1)} custom-call(f32[128,128]{1,0:T(8,128)S(1)} %fusion.24), custom_call_target="Cholesky" | custom-call | tf_op jit(solution)/shard_map/jit(cholesky)/cholesky | solution.py:130
  163.9 0.7 compare_reduce_fusion
  164.6 0.6 fusion.17
  165.3 9.8 %custom-call.8 = f32[1,128,128]{1,2,0:T(8,128)S(1)} custom-call(f32[1,128,128]{2,1,0:T(8,128)S(1)} %fusion.17), custom_call_target="InvertDiagBlocksLowerTriangular" | custom-call | tf_op jit(solution)/shard_map/triangular_solve | solution.py:132
  175.1 1.1 fusion.22
  176.5 43.0 %all-gather.2.cloned.1.call-done = f32[128,12288]{1,0:T(8,128)} async-done(((f32[16,12288]{1,0:T(8,128)}), f32[128,12288]{1,0:T(8,128)}) %all-gather.2.cloned.1.call-update) | async-done | bytes 6291472 | tf_op jit(solution)/shard_map/all_gather | solution.py:144
  219.6 5.2 %convolution_bitcast_fusion = f32[2,8,96,128]{3,1,2,0:T(8,128)S(1)} fusion(f32[128,12288]{1,0:T(8,128)} %all-gather.2.cloned.1.call-done, f32[128,128]{1,0:T(8,128)S(1)} %get-tuple-element.24, s32[]{:T(128)S(6)} %select_n.60, f32[128,128]{1,0:T(8,128)S(1)} %fusion.25, f32[16]{0:T(128)S(1)} %dynamic-slice), kind=kOutput, calls=%fused_computation.15 | convolution fusion | flops 301993984 | bytes 7209028 | tf_op jit(solution)/shard_map/dot_general | solution.py:142
  224.8 1.0 copy.37
  (36 shorter events, 1.2 us)
Async XLA Ops:
  7.4 47.1 %reduce-scatter.2.cloned.1.call-start = ((), (), s32[]{:S(2)}) async-start(), calls=%async_computation.1 | async-start | bytes 81920 | tf_op jit(solution)/shard_map/reduce_scatter | solution.py:118
  9.0 4.6 %collective-permute-start = (f32[16,3,4,1,128]{4,0,3,2,1:T(8,128)S(1)}, f32[16,3,4,1,128]{4,0,3,2,1:T(8,128)S(1)}, u32[]{:S(2)}, u32[]{:S(2)}) collective-permute-start(f32[16,3,4,1,128]{4,0,3,2,1:T(8,128)S(1)} %copy.34), channel_id=1, source_target_pairs={{0,1},{1,2},{2,3},{4,5},{5,6},{6,7},{8,9},{9,10},{10,11},{12,13},{... | collective-permute-start | bytes 294920 | tf_op jit(solution)/shard_map/ppermute | solution.py:23
  11.4 5.3 %collective-permute-start.1 = (f32[16,3,4,1,128]{4,0,3,2,1:T(8,128)S(1)}, f32[16,3,4,1,128]{4,0,3,2,1:T(8,128)S(1)}, u32[]{:S(2)}, u32[]{:S(2)}) collective-permute-start(f32[16,3,4,1,128]{4,0,3,2,1:T(8,128)S(1)} %copy.35), channel_id=1, source_target_pairs={{1,0},{2,1},{3,2},{5,4},{6,5},{7,6},{9,8},{10,9},{11,10},{13,12},{... | collective-permute-start | bytes 294920 | tf_op jit(solution)/shard_map/ppermute | solution.py:25
  23.0 8.6 %copy-start.1 = (f32[256]{0:T(256)S(1)}, f32[256]{0:T(256)}, u32[]{:S(2)}) copy-start(f32[256]{0:T(256)} %param.8) | copy-start | bytes 3076
  23.0 62.3 %copy-start = (f32[256,16]{0,1:T(8,128)S(1)}, f32[256,16]{0,1:T(8,128)}, u32[]{:S(2)}) copy-start(f32[256,16]{0,1:T(8,128)} %param.9) | copy-start | bytes 49156
  23.0 62.3 %copy-start.2 = (f32[256]{0:T(256)S(1)}, f32[256]{0:T(256)}, u32[]{:S(2)}) copy-start(f32[256]{0:T(256)} %param.7) | copy-start | bytes 3076
  23.0 95.6 %slice-start = ((f32[16,3,4,8,128]{4,3,2,1,0:T(8,128)}), f32[16,1,4,8,128]{4,3,2,1,0:T(8,128)S(1)}, s32[]{:S(2)}) async-start(f32[16,3,4,8,128]{4,3,2,1,0:T(8,128)} %param.5), calls=%async_computation.4 | async-start | bytes 524288 | tf_op jit(solution)/shard_map/slice | solution.py:100
  31.5 118.8 %all-reduce.4.cloned.1.call-start = ((), (), s32[]{:S(2)}) async-start(), calls=%async_computation.3 | async-start | bytes 262144 | tf_op jit(solution)/shard_map/psum | solution.py:128
  118.4 101.2 %all-gather.2.cloned.1.call-start = ((), (), s32[]{:S(2)}) async-start(), calls=%async_computation.2 | async-start | bytes 7077888 | tf_op jit(solution)/shard_map/all_gather | solution.py:144
Sparse Core Ops, SparseCore 0:
  31.6 22.7 reduce-scatter.1
  118.5 31.8 all-reduce.3
Sparse Core Ops, SparseCore 1:
  121.0 98.5 all-gather.1
where the time goes:
time: 234 us; the launch traced here: 233 us
  waiting for transfers between devices  99.2 us (42%)
  blocking collectives  61.3 us (26%)
  other arithmetic  32.8 us (14%)
  between operations  15.2 us (6%)
  local copies, waits for them, and re-layouts  12.5 us (5%)
  matrix products  8.35 us (4%)
  starting transfers between devices  3.96 us (2%)
    all_gather x1, waiting for transfers between devices, local(): lax.all_gather(raveled_trial_vector, 'mem', axis=0, tiled=True)  43 us
    all_gather x1, blocking collectives, local(): lax.all_gather(own_data, 'mem', axis=0, tiled=True)  30.8 us
    all_gather x1, blocking collectives, local(): lax.all_gather(innovation, 'mem', axis=0, tiled=True)  30.5 us
    psum x1, waiting for transfers between devices, local(): gram_sum, cross_sum = lax.psum((gram_part, cross_part), 'tile')  30.3 us
    reduce_scatter x1, waiting for transfers between devices, local(): lax.psum_scatter(partial_data, 'tile', scatter_dimension=1, tiled=True)  22.8 us
    another operation x3, other arithmetic, local(): lower_factor = jnp.linalg.cholesky(identity + gram_sum)  12.5 us
    another operation x2, other arithmetic, local(): lax.linalg.triangular_solve(lower_factor, half_solve, left_side=True, low...  10.5 us
    dot_general x1, matrix products, local(): jnp.dot(own_columns.T, lax.all_gather(raveled_trial_vector, 'mem', axis=0...  5.2 us
  transfers between devices with their start and end apart: 5, of which 4 were waited for; matrix products, arithmetic and copies ran while one was open for 12% of the time, Pallas kernels for 0%

commit v1 on v0

v1 whole, which is shorter than its diff:
```python
import functools
import math

import jax
import jax.numpy as jnp
from jax import lax
from jax.experimental import pallas as pl
from jax.experimental.pallas import tpu as pltpu
from jax.sharding import PartitionSpec as P

alpha_mda = 4.0
buoyancy = 0.5
head_rate = 0.02
salt_diffusion = 0.01
salt_advection = 0.01
HI = lax.Precision.HIGHEST
MESH = pl.DeviceIdType.MESH
VM = pl.BlockSpec(memory_space=pltpu.VMEM)


def forecast_kernel(x_ref, up_ref, dn_ref, row_ref, col_ref, fc_ref, pred_ref, k_ref):
    fields, layers, width, members, lanes = x_ref.shape
    groups = row_ref.shape[0]
    rank = lax.axis_index("tile")
    last = lax.axis_size("tile") - 1
    has_up = jnp.where(rank > 0, 1.0, 0.0).astype(jnp.float32)
    has_dn = jnp.where(rank < last, 1.0, 0.0).astype(jnp.float32)
    for l in range(layers):
        k_ref[l, 0] = jnp.exp(up_ref[0, l]) * has_up
        k_ref[l, width + 1] = jnp.exp(dn_ref[0, l]) * has_dn
        for r in range(width):
            k_ref[l, r + 1] = jnp.exp(x_ref[0, l, r])
    lane = lax.broadcasted_iota(jnp.int32, (members, lanes), 1)

    def cell(f, l, r):
        if r < 0:
            return up_ref[f, l]
        if r >= width:
            return dn_ref[f, l]
        return x_ref[f, l, r]

    def layer_row(l, r):
        k0, h0, c0 = k_ref[l, r + 1], x_ref[1, l, r], x_ref[2, l, r]
        hs = jnp.zeros_like(h0)
        cs = jnp.zeros_like(c0)
        near = []
        if l > 0:
            near.append((-1.0, k_ref[l - 1, r + 1], cell(1, l - 1, r), cell(2, l - 1, r)))
        if l < layers - 1:
            near.append((1.0, k_ref[l + 1, r + 1], cell(1, l + 1, r), cell(2, l + 1, r)))
        near.append((0.0, k_ref[l, r], cell(1, l, r - 1), cell(2, l, r - 1)))
        near.append((0.0, k_ref[l, r + 2], cell(1, l, r + 1), cell(2, l, r + 1)))
        near.append(
            (
                0.0,
                jnp.where(lane == 0, 0.0, pltpu.roll(k0, 1, 1)),
                pltpu.roll(h0, 1, 1),
                pltpu.roll(c0, 1, 1),
            )
        )
        near.append(
            (
                0.0,
                jnp.where(lane == lanes - 1, 0.0, pltpu.roll(k0, lanes - 1, 1)),
                pltpu.roll(h0, lanes - 1, 1),
                pltpu.roll(c0, lanes - 1, 1),
            )
        )
        for s, kn, hn, cn in near:
            g = 2.0 * k0 * kn / (k0 + kn)
            csum = c0 + cn
            drop = hn - h0
            if s != 0.0:
                drop = drop + (s * buoyancy * 0.5) * csum
            flux = g * drop
            hs = hs + flux
            cs = cs + salt_diffusion * g * (cn - c0) + salt_advection * flux * 0.5 * csum
        flat = l * width + r
        per = layers * width
        fc_ref[flat] = x_ref[0, l, r]
        fc_ref[per + flat] = h0 + head_rate * hs
        fc_ref[2 * per + flat] = c0 + cs

    for l in range(layers):
        for r in range(width):
            layer_row(l, r)
    rows = [jnp.broadcast_to(row_ref[g], (members, lanes)) for g in range(groups)]
    cols = [jnp.broadcast_to(col_ref[g], (members, lanes)) for g in range(groups)]
    per = layers * width
    step = 8
    for g0 in range(0, groups, step):
        part = range(g0, min(g0 + step, groups))

        def body(r, accs):
            v = fc_ref[per + r]
            return tuple(
                jnp.where(rows[g] == r, jnp.take_along_axis(v, cols[g], axis=1), a)
                for g, a in zip(part, accs)
            )

        accs = lax.fori_loop(
            0, 2 * per, body, tuple(jnp.zeros((members, lanes), jnp.float32) for _ in part)
        )
        for g, a in zip(part, accs):
            pred_ref[g] = a


def analysis_kernel(
    fc_ref, pred_ref, noise_ref, obs_ref, scale_ref, out_ref,
    pbuf, nbuf, part, rsbuf, gc, gbuf, obuf, sref, cref,
    s_pred, r_pred, s_noise, r_noise, s_fwd, r_fwd, s_rs, r_rs, s_ag, r_ag, s_back, r_back, s_loc,
):
    nm, nt = lax.axis_size("mem"), lax.axis_size("tile")
    n = nm * nt
    d, t = lax.axis_index("mem"), lax.axis_index("tile")
    me = d * nt + t
    gpc, members, lanes = pbuf.shape[2:]
    ncl = nm // nt
    total = nm * members
    reducers, blk, blk_lanes = gc.shape
    crows = gbuf.shape[0]
    worker = t == d // ncl

    def remote(src, dst, ss, rs, mem, tile):
        return pltpu.make_async_remote_copy(
            src_ref=src, dst_ref=dst, send_sem=ss, recv_sem=rs,
            device_id={"mem": mem, "tile": tile}, device_id_type=MESH,
        )

    def drain(ref, sem):
        pltpu.make_async_copy(ref, ref, sem).wait()

    barrier = pltpu.get_barrier_semaphore()

    def greet(i, _):
        to = lax.rem(me + i, n)
        pl.semaphore_signal(
            barrier, 1, device_id={"mem": to // nt, "tile": lax.rem(to, nt)}, device_id_type=MESH
        )
        return 0

    lax.fori_loop(1, n, greet, 0)
    pl.semaphore_wait(barrier, n - 1)

    for k in range(nm):
        c = lax.rem(d + k, nm)
        src = pred_ref.at[pl.ds(c * gpc, gpc)]
        if k == 0:
            @pl.when(worker)
            def _():
                pbuf[t, d] = pred_ref[pl.ds(d * gpc, gpc)]

            @pl.when(jnp.logical_not(worker))
            def _():
                remote(src, pbuf.at[t, d], s_pred, r_pred, c, c // ncl).start()
        else:
            remote(src, pbuf.at[t, d], s_pred, r_pred, c, c // ncl).start()
    for j in range(ncl):
        c = t * ncl + j
        src = noise_ref.at[pl.ds(j * gpc, gpc)]

        @pl.when(c != d)
        def _():
            remote(src, nbuf.at[d], s_noise, r_noise, c, t).start()

        @pl.when(c == d)
        def _():
            nbuf[d] = noise_ref[pl.ds(j * gpc, gpc)]

    mine = pl.ds(pl.multiple_of(d * members, members), members)
    for k in range(1, nm):
        c = lax.rem(d + k, nm)
        remote(
            fc_ref.at[pl.ds(c * crows, crows)], gbuf.at[:, mine, :], s_fwd, r_fwd, c, t
        ).start()
    local = pltpu.make_async_copy(
        fc_ref.at[pl.ds(d * crows, crows)], gbuf.at[:, mine, :], s_loc
    )
    local.start()

    @pl.when(worker)
    def _():
        drain(pbuf_flat(pbuf, n - 1), r_pred)
        drain(nbuf.at[pl.ds(0, nm - 1)], r_noise)
        gram = jnp.zeros((total, total), jnp.float32)
        cross = jnp.zeros((total, total), jnp.float32)
        base = lax.rem(d, ncl) * gpc
        for g in range(gpc):
            pred = pbuf[0, :, g]
            for q in range(1, nt):
                pred = pred + pbuf[q, :, g]
            pred = pred.reshape(total, lanes)
            noise = nbuf[:, g].reshape(total, lanes)
            scale = scale_ref[base + g]
            innov = (obs_ref[base + g] - pred) / scale + noise
            anom = (pred - jnp.mean(pred, axis=0, keepdims=True)) / (
                scale * math.sqrt(total - 1)
            )
            dims = (((1,), (1,)), ((), ()))
            gram = gram + lax.dot_general(
                anom, anom, dims, precision=HI, preferred_element_type=jnp.float32
            )
            cross = cross + lax.dot_general(
                anom, innov, dims, precision=HI, preferred_element_type=jnp.float32
            )
        half = reducers // 2
        part[pl.ds(0, half)] = gram.reshape(half, blk, blk_lanes)
        part[pl.ds(half, half)] = cross.reshape(half, blk, blk_lanes)

        def scatter(i, _):
            to = lax.rem(me + i, n)

            @pl.when(to < reducers)
            def _():
                remote(part.at[to], rsbuf.at[d], s_rs, r_rs, to // nt, lax.rem(to, nt)).start()
            return 0

        lax.fori_loop(1, n, scatter, 0)

        @pl.when(me < reducers)
        def _():
            rsbuf[d] = part[me]

    @pl.when(me < reducers)
    def _():
        @pl.when(worker)
        def _():
            drain(rsbuf.at[pl.ds(0, nm - 1)], r_rs)

        @pl.when(jnp.logical_not(worker))
        def _():
            drain(rsbuf, r_rs)
        acc = rsbuf[0]
        for q in range(1, nm):
            acc = acc + rsbuf[q]
        gc[me] = acc

        def spread(i, _):
            to = lax.rem(me + i, n)
            remote(gc.at[me], gc.at[me], s_ag, r_ag, to // nt, lax.rem(to, nt)).start()
            return 0

        lax.fori_loop(1, n, spread, 0)
        drain(gc.at[pl.ds(0, reducers - 1)], r_ag)

    if reducers < n:
        @pl.when(me >= reducers)
        def _():
            drain(gc, r_ag)

    half = reducers // 2
    eye = (
        lax.broadcasted_iota(jnp.int32, (total, total), 0)
        == lax.broadcasted_iota(jnp.int32, (total, total), 1)
    ).astype(jnp.float32)
    sref[...] = gc[pl.ds(0, half)].reshape(total, total) + eye
    cref[...] = gc[pl.ds(half, half)].reshape(total, total)
    b = 16
    blane = lax.broadcasted_iota(jnp.int32, (b, total), 1)
    brow = lax.broadcasted_iota(jnp.int32, (b, total), 0)
    flane = lax.broadcasted_iota(jnp.int32, (total, total), 1)

    def sweep(g, _):
        first = pl.multiple_of(g * b, b)
        rows = sref[pl.ds(first, b), :]
        z_c = cref[pl.ds(first, b), :]
        piv = pltpu.roll(rows, lax.rem(total - first, total), 1)
        own = (blane >= first) & (blane < first + b)
        z_s = jnp.where(own, jnp.where(blane == brow + first, -1.0, 0.0), rows)
        for k in range(b):
            inv = 1.0 / piv[k : k + 1, k : k + 1]
            col = piv[:, k : k + 1]
            fac = jnp.where(brow == k, 0.0, col)
            at = brow == k

            def upd(z):
                new = z[k : k + 1, :] * inv
                return jnp.where(at, new, z - fac * new)

            piv, z_s, z_c = upd(piv), upd(z_s), upd(z_c)
        left = rows.T
        keep = (flane >= first) & (flane < first + b)
        s_old = jnp.where(keep, 0.0, sref[...])
        s_new = s_old - jnp.dot(left, z_s, precision=HI, preferred_element_type=jnp.float32)
        c_new = cref[...] - jnp.dot(left, z_c, precision=HI, preferred_element_type=jnp.float32)
        sref[...] = s_new
        cref[...] = c_new
        sref[pl.ds(first, b), :] = z_s
        cref[pl.ds(first, b), :] = z_c
        return 0

    lax.fori_loop(0, total // b, sweep, 0)
    scaled = cref[...] / math.sqrt(total - 1)
    mix = (eye + scaled - jnp.mean(scaled, axis=0, keepdims=True)).T

    local.wait()
    drain(gbuf.at[:, pl.ds(0, (nm - 1) * members), :], r_fwd)
    parts = 3 if crows % 3 == 0 else 1
    pr = crows // parts
    for q in range(parts):
        for r in range(q * pr, (q + 1) * pr):
            obuf[r] = jnp.dot(mix, gbuf[r], precision=HI, preferred_element_type=jnp.float32)
        for k in range(1, nm):
            c = lax.rem(d + k, nm)
            theirs = pl.ds(pl.multiple_of(c * members, members), members)
            remote(
                obuf.at[pl.ds(q * pr, pr), theirs, :],
                out_ref.at[pl.ds(d * crows + q * pr, pr)],
                s_back, r_back, c, t,
            ).start()
    out_ref[pl.ds(d * crows, crows)] = obuf[:, mine, :]

    @pl.when(worker)
    def _():
        drain(pred_ref.at[pl.ds(0, (nm - 1) * gpc)], s_pred)
        if reducers < n:
            @pl.when(me < reducers)
            def _():
                drain(part.at[pl.ds(0, reducers - 1)], s_rs)

            @pl.when(me >= reducers)
            def _():
                drain(part, s_rs)
        else:
            drain(part.at[pl.ds(0, reducers - 1)], s_rs)

    @pl.when(jnp.logical_not(worker))
    def _():
        drain(pred_ref, s_pred)

    @pl.when(worker)
    def _():
        if ncl > 1:
            drain(noise_ref.at[pl.ds(0, (ncl - 1) * gpc)], s_noise)

    @pl.when(jnp.logical_not(worker))
    def _():
        drain(noise_ref, s_noise)

    @pl.when(me < reducers)
    def _():
        def done(i, _):
            drain(gc.at[0], s_ag)
            return 0

        if reducers == n:
            drain(gc.at[pl.ds(0, n - 1)], s_ag)
        else:
            lax.fori_loop(1, n, done, 0)
    drain(fc_ref.at[pl.ds(0, (nm - 1) * crows)], s_fwd)
    drain(obuf.at[:, pl.ds(0, (nm - 1) * members), :], s_back)
    drain(out_ref.at[pl.ds(0, (nm - 1) * crows)], r_back)


def pbuf_flat(ref, count):
    nt, nm = ref.shape[:2]
    return ref.reshape((nt * nm,) + ref.shape[2:]).at[pl.ds(0, count)]


def local(fields_in, offsets, observed, obs_var, obs_noise):
    members, fields, layers, width, lanes = fields_in.shape
    rank = lax.axis_index("tile")
    nt, nm = lax.axis_size("tile"), lax.axis_size("mem")
    n = nt * nm
    x = fields_in.transpose(1, 2, 3, 0, 4)
    up = lax.ppermute(x[:, :, width - 1], "tile", [(i, i + 1) for i in range(nt - 1)])
    dn = lax.ppermute(x[:, :, 0], "tile", [(i + 1, i) for i in range(nt - 1)])
    plane = width * nt * lanes
    lay = offsets // plane
    rest = offsets % plane
    lrow = rest // lanes - rank * width
    row = jnp.where((lrow >= 0) & (lrow < width), lay * width + lrow, -1)
    groups = offsets.shape[0] // lanes
    row = row.reshape(groups, 1, lanes)
    col = (rest % lanes).reshape(groups, 1, lanes)
    rows = fields * layers * width
    f32 = jnp.float32
    fc, pred = pl.pallas_call(
        forecast_kernel,
        out_shape=(
            jax.ShapeDtypeStruct((rows, members, lanes), f32),
            jax.ShapeDtypeStruct((groups, members, lanes), f32),
        ),
        in_specs=[VM] * 5,
        out_specs=(VM, VM),
        scratch_shapes=[pltpu.VMEM((layers, width + 2, members, lanes), f32)],
    )(x, up, dn, row, col)
    gpc = groups // nm
    own = groups // nt
    noise = obs_noise.reshape(own, lanes, members).transpose(0, 2, 1)
    obs = observed.reshape(own, 1, lanes)
    scale = jnp.sqrt(alpha_mda * obs_var).reshape(own, 1, lanes)
    total = members * nm
    reducers = min(n, 2 * total // 8)
    blk = 2 * total // reducers
    crows = rows // nm
    dma = pltpu.SemaphoreType.DMA
    out = pl.pallas_call(
        analysis_kernel,
        out_shape=jax.ShapeDtypeStruct((rows, members, lanes), f32),
        in_specs=[VM] * 5,
        out_specs=VM,
        scratch_shapes=[
            pltpu.VMEM((nt, nm, gpc, members, lanes), f32),
            pltpu.VMEM((nm, gpc, members, lanes), f32),
            pltpu.VMEM((reducers, blk, total), f32),
            pltpu.VMEM((nm, blk, total), f32),
            pltpu.VMEM((reducers, blk, total), f32),
            pltpu.VMEM((crows, total, lanes), f32),
            pltpu.VMEM((crows, total, lanes), f32),
            pltpu.VMEM((total, total), f32),
            pltpu.VMEM((total, total), f32),
        ]
        + [dma] * 13,
        compiler_params=pltpu.CompilerParams(collective_id=0, has_side_effects=True),
    )(fc, pred, noise, obs, scale)
    return out.reshape(fields, layers, width, members, lanes).transpose(3, 0, 1, 2, 4)


def solution(mesh):
    in_specs = (P("mem", None, None, "tile", None), P(), P("tile"), P("tile"), P("tile", "mem"))
    out_specs = P("mem", None, None, "tile", None)
    return jax.shard_map(local, mesh=mesh, in_specs=in_specs, out_specs=out_specs, check_vma=False)
```

time: 234 us -> 90.8 us (0.39)
  waiting for transfers between devices: 99.2 us -> 0.65 us
  Pallas kernels: 0 us -> 78.2 us
  blocking collectives: 61.3 us -> 0 us
  other arithmetic: 32.8 us -> 1.21 us
  between operations: 15.2 us -> 0.06 us
  matrix products: 8.35 us -> 0 us
  local copies, waits for them, and re-layouts: 12.5 us -> 6.68 us
    pallas_call x0 -> x2, Pallas kernels: none -> 78.2 us  [the longest x1 68.6 us: local(): pl.pallas_call(analysis_kernel, out_shape=jax.ShapeDtypeStruct((rows, mem...]
    all_gather x2 -> x0, blocking collectives: 61.3 us -> none  [the longest x1 30.8 us: local(): lax.all_gather(own_data, 'mem', axis=0, tiled=True)]
    all_gather x1 -> x0, waiting for transfers between devices: 43 us -> none  [local(): lax.all_gather(raveled_trial_vector, 'mem', axis=0, tiled=True)]
    psum x1 -> x0, waiting for transfers between devices: 30.3 us -> none  [local(): gram_sum, cross_sum = lax.psum((gram_part, cross_part), 'tile')]
    another operation x9 -> x0, other arithmetic: 25.4 us -> none  [the longest x3 12.5 us: local(): lower_factor = jnp.linalg.cholesky(identity + gram_sum)]
    reduce_scatter x1 -> x0, waiting for transfers between devices: 22.8 us -> none  [local(): lax.psum_scatter(partial_data, 'tile', scatter_dimension=1, tiled=True)]
    dot_general x3 -> x0, matrix products: 7 us -> none  [the longest x1 5.2 us: local(): jnp.dot(own_columns.T, lax.all_gather(raveled_trial_vector, 'mem', axis=0...]
    gather x2 -> x0, local copies, waits for them, and re-layouts: 5.16 us -> none  [local(): values = jnp.take(raveled_measured_vector, local_index, axis=1)]
  transfers between devices with their start and end apart: 5 -> 2, of which waited for: 4 -> 1; matrix products, arithmetic and copies ran while one was open for 12% -> 3% of each run, Pallas kernels for 0% -> 0%
where the time goes in v1:
time: 90.8 us; the launch traced here: 90.5 us
  Pallas kernels  78.2 us (86%)
  local copies, waits for them, and re-layouts  6.68 us (7%)
  starting transfers between devices  3.69 us (4%)
  other arithmetic  1.21 us (1%)
    pallas_call x1, Pallas kernels, local(): pl.pallas_call(analysis_kernel, out_shape=jax.ShapeDtypeStruct((rows, mem...  68.6 us
    pallas_call x1, Pallas kernels, local(): pl.pallas_call(forecast_kernel, out_shape=(jax.ShapeDtypeStruct((rows, me...  9.53 us
    unnamed x13, local copies, waits for them, and re-layouts  2.46 us
    ppermute x1, starting transfers between devices, local(): lax.ppermute(x[:, :, width - 1], 'tile', [(i, i + 1) for i in range(nt -...  2.4 us
    reshape x1, local copies, waits for them, and re-layouts, local(): out.reshape(fields, layers, width, members, lanes).transpose(3, 0, 1, 2, 4)  2.27 us
  transfers between devices with their start and end apart: 2, of which 1 were waited for; matrix products, arithmetic and copies ran while one was open for 3% of the time, Pallas kernels for 0%

profile of v1, /device:TPU:0, one launch (start us, length us, event | category | flops | bytes accessed | tf_op | source)
XLA Modules:
  0.0 90.5 jit_solution(5003579041363304677)
XLA Ops:
  0.0 0.0 copy-start
  0.0 0.0 copy-start.1
  0.0 1.7 %copy.19 = f32[16,3,4,8,128]{4,0,2,1,3:T(8,128)S(1)} copy(f32[16,3,4,8,128]{4,3,2,1,0:T(8,128)} %param.5) | data formatting | bytes 1572864 | tf_op args[0]
  1.7 2.4 %collective-permute-start = (f32[3,4,16,128]{3,2,1,0:T(8,128)S(1)}, f32[3,4,16,128]{3,2,1,0:T(8,128)S(1)}, u32[]{:S(2)}, u32[]{:S(2)}) collective-permute-start(f32[3,4,16,128]{3,2,1,0:T(8,128)S(1)} %get-tuple-element.10), channel_id=1, source_target_pairs={{0,1},{1,2},{2,3},{4,5},{5,6},{6,7},{8,9},{9,10},{10,11},{12,13},{... | collective-permute-start | bytes 294920 | tf_op jit(solution)/shard_map/ppermute | solution.py:366
  4.1 1.3 %collective-permute-start.1 = (f32[3,4,16,128]{3,2,1,0:T(8,128)S(1)}, f32[3,4,16,128]{3,2,1,0:T(8,128)S(1)}, u32[]{:S(2)}, u32[]{:S(2)}) collective-permute-start(f32[3,4,16,128]{3,2,1,0:T(8,128)S(1)} %get-tuple-element.9), channel_id=1, source_target_pairs={{1,0},{2,1},{3,2},{5,4},{6,5},{7,6},{9,8},{10,9},{11,10},{13,12},{... | collective-permute-start | bytes 294920 | tf_op jit(solution)/shard_map/ppermute | solution.py:367
  5.4 0.0 copy-done
  5.4 0.0 copy-start.4
  5.4 0.6 bitcast_bitcast_fusion.noise_ref
  6.0 0.1 copy-done.4
  6.1 0.0 copy-start.5
  6.1 0.6 add_select_fusion
  6.7 0.1 copy-done.5
  6.8 0.6 multiply_sqrt_fusion
  7.4 0.0 copy-done.1
  7.4 1.3 %copy.10.x_ref = f32[3,4,8,16,128]{4,3,2,1,0:T(8,128)} copy(f32[3,4,8,16,128]{4,2,1,0,3:T(8,128)S(1)} %bitcast.23) | data formatting | bytes 1572864 | tf_op jit(solution)/shard_map/transpose | solution.py:365
  8.7 0.0 collective-permute-done.up_ref
  8.7 0.0 copy-start.2
  8.7 0.7 collective-permute-done.1.dn_ref
  9.4 0.0 copy-start.3
  9.4 0.0 copy-done.2
  9.4 0.6 copy-done.3
  10.0 9.5 %shard_map.55 = (f32[96,16,128]{2,1,0:T(8,128)}, f32[8,16,128]{2,1,0:T(8,128)}) custom-call(f32[3,4,8,16,128]{4,3,2,1,0:T(8,128)} %copy.10.x_ref, f32[3,4,16,128]{3,2,1,0:T(8,128)} %copy-done.2, f32[3,4,16,128]{3,2,1,0:T(8,128)} %copy-done.3, s32[8,1,128]{2,1,0:T(1,128)} %bitcast.27, s32[8,1,128]{2,1,0:T(1,128)} %bitcast.26), custom_call_target="tpu_custom_call" | custom-call | tf_op jit(solution)/shard_map/pallas_call | solution.py:378
  19.6 68.6 %shard_map.56 = f32[96,16,128]{2,1,0:T(8,128)} custom-call(f32[96,16,128]{2,1,0:T(8,128)} %get-tuple-element.7.fc_ref, f32[8,16,128]{2,1,0:T(8,128)} %get-tuple-element.8.pred_ref, f32[2,16,128]{2,1,0:T(8,128)} %bitcast_bitcast_fusion.noise_ref, f32[2,1,128]{2,1,0:T(1,128)} %bitcast.29, f32[2,1,128]{2,1,0:T(1,128)} %bitcast.28), custom_call_target="tpu_custom_call" | custom-call | tf_op jit(solution)/shard_map/pallas_call | solution.py:398
  88.2 2.3 %copy.18 = f32[3,4,8,16,128]{4,2,1,0,3:T(8,128)} copy(f32[3,4,8,16,128]{4,3,2,1,0:T(8,128)} %bitcast.24) | data formatting | bytes 1572864 | tf_op jit(solution)/shard_map/reshape | solution.py:417
  (1 shorter events, 0.0 us)
Async XLA Ops:
  0.0 5.4 %copy-start = (f32[256,16]{0,1:T(8,128)S(1)}, f32[256,16]{0,1:T(8,128)}, u32[]{:S(2)}) copy-start(f32[256,16]{0,1:T(8,128)} %param.9) | copy-start | bytes 49156
  0.0 7.4 %copy-start.1 = (f32[16,3,4,8,128]{4,3,2,1,0:T(8,128)S(1)}, f32[16,3,4,8,128]{4,3,2,1,0:T(8,128)}, u32[]{:S(2)}) copy-start(f32[16,3,4,8,128]{4,3,2,1,0:T(8,128)} %param.5) | copy-start | bytes 2359300
  1.7 7.0 %collective-permute-start = (f32[3,4,16,128]{3,2,1,0:T(8,128)S(1)}, f32[3,4,16,128]{3,2,1,0:T(8,128)S(1)}, u32[]{:S(2)}, u32[]{:S(2)}) collective-permute-start(f32[3,4,16,128]{3,2,1,0:T(8,128)S(1)} %get-tuple-element.10), channel_id=1, source_target_pairs={{0,1},{1,2},{2,3},{4,5},{5,6},{6,7},{8,9},{9,10},{10,11},{12,13},{... | collective-permute-start | bytes 294920 | tf_op jit(solution)/shard_map/ppermute | solution.py:366
  4.1 5.3 %collective-permute-start.1 = (f32[3,4,16,128]{3,2,1,0:T(8,128)S(1)}, f32[3,4,16,128]{3,2,1,0:T(8,128)S(1)}, u32[]{:S(2)}, u32[]{:S(2)}) collective-permute-start(f32[3,4,16,128]{3,2,1,0:T(8,128)S(1)} %get-tuple-element.9), channel_id=1, source_target_pairs={{1,0},{2,1},{3,2},{5,4},{6,5},{7,6},{9,8},{10,9},{11,10},{13,12},{... | collective-permute-start | bytes 294920 | tf_op jit(solution)/shard_map/ppermute | solution.py:367
  5.4 0.7 copy-start.4
  6.1 0.7 copy-start.5
  8.7 0.7 copy-start.2
  9.4 0.6 copy-start.3

commit v2 on v1

--- a/solution.py
+++ b/solution.py
@@ -18,75 +18,75 @@
 VM = pl.BlockSpec(memory_space=pltpu.VMEM)
 
 
-def forecast_kernel(x_ref, up_ref, dn_ref, row_ref, col_ref, fc_ref, pred_ref, k_ref):
+def face(a, b, buoyant):
+    ka, ha, ca = a
+    kb, hb, cb = b
+    g = 2.0 * ka * kb / (ka + kb)
+    csum = ca + cb
+    drop = hb - ha
+    if buoyant:
+        drop = drop + (buoyancy * 0.5) * csum
+    flux = g * drop
+    return flux, salt_diffusion * g * (cb - ca) + (salt_advection * 0.5) * flux * csum
+
+
+def step_inside(x_ref, fc_ref, k_ref, lay_ref):
     fields, layers, width, members, lanes = x_ref.shape
-    groups = row_ref.shape[0]
-    rank = lax.axis_index("tile")
-    last = lax.axis_size("tile") - 1
-    has_up = jnp.where(rank > 0, 1.0, 0.0).astype(jnp.float32)
-    has_dn = jnp.where(rank < last, 1.0, 0.0).astype(jnp.float32)
+    per = layers * width
+    lane = lax.broadcasted_iota(jnp.int32, (members, lanes), 1)
     for l in range(layers):
-        k_ref[l, 0] = jnp.exp(up_ref[0, l]) * has_up
-        k_ref[l, width + 1] = jnp.exp(dn_ref[0, l]) * has_dn
         for r in range(width):
-            k_ref[l, r + 1] = jnp.exp(x_ref[0, l, r])
-    lane = lax.broadcasted_iota(jnp.int32, (members, lanes), 1)
-
-    def cell(f, l, r):
-        if r < 0:
-            return up_ref[f, l]
-        if r >= width:
-            return dn_ref[f, l]
-        return x_ref[f, l, r]
-
-    def layer_row(l, r):
-        k0, h0, c0 = k_ref[l, r + 1], x_ref[1, l, r], x_ref[2, l, r]
-        hs = jnp.zeros_like(h0)
-        cs = jnp.zeros_like(c0)
-        near = []
-        if l > 0:
-            near.append((-1.0, k_ref[l - 1, r + 1], cell(1, l - 1, r), cell(2, l - 1, r)))
-        if l < layers - 1:
-            near.append((1.0, k_ref[l + 1, r + 1], cell(1, l + 1, r), cell(2, l + 1, r)))
-        near.append((0.0, k_ref[l, r], cell(1, l, r - 1), cell(2, l, r - 1)))
-        near.append((0.0, k_ref[l, r + 2], cell(1, l, r + 1), cell(2, l, r + 1)))
-        near.append(
-            (
-                0.0,
-                jnp.where(lane == 0, 0.0, pltpu.roll(k0, 1, 1)),
-                pltpu.roll(h0, 1, 1),
-                pltpu.roll(c0, 1, 1),
-            )
-        )
-        near.append(
-            (
-                0.0,
+            k_ref[l, r] = jnp.exp(x_ref[0, l, r])
+    for l in range(layers):
+        row_face = None
+        for r in range(width):
+            here = (k_ref[l, r], x_ref[1, l, r], x_ref[2, l, r])
+            k0, h0, c0 = here
+            right = (
                 jnp.where(lane == lanes - 1, 0.0, pltpu.roll(k0, lanes - 1, 1)),
                 pltpu.roll(h0, lanes - 1, 1),
                 pltpu.roll(c0, lanes - 1, 1),
             )
-        )
-        for s, kn, hn, cn in near:
-            g = 2.0 * k0 * kn / (k0 + kn)
-            csum = c0 + cn
-            drop = hn - h0
-            if s != 0.0:
-                drop = drop + (s * buoyancy * 0.5) * csum
-            flux = g * drop
-            hs = hs + flux
-            cs = cs + salt_diffusion * g * (cn - c0) + salt_advection * flux * 0.5 * csum
-        flat = l * width + r
-        per = layers * width
-        fc_ref[flat] = x_ref[0, l, r]
-        fc_ref[per + flat] = h0 + head_rate * hs
-        fc_ref[2 * per + flat] = c0 + cs
-
+            fh, fs = face(here, right, False)
+            hs, cs = fh - pltpu.roll(fh, 1, 1), fs - pltpu.roll(fs, 1, 1)
+            if row_face is not None:
+                hs, cs = hs - row_face[0], cs - row_face[1]
+            if r < width - 1:
+                row_face = face(
+                    here, (k_ref[l, r + 1], x_ref[1, l, r + 1], x_ref[2, l, r + 1]), False
+                )
+                hs, cs = hs + row_face[0], cs + row_face[1]
+            if l > 0:
+                hs, cs = hs - lay_ref[0, r], cs - lay_ref[1, r]
+            if l < layers - 1:
+                fh, fs = face(here, (k_ref[l + 1, r], x_ref[1, l + 1, r], x_ref[2, l + 1, r]), True)
+                lay_ref[0, r] = fh
+                lay_ref[1, r] = fs
+                hs, cs = hs + fh, cs + fs
+            flat = l * width + r
+            fc_ref[flat] = x_ref[0, l, r]
+            fc_ref[per + flat] = h0 + head_rate * hs
+            fc_ref[2 * per + flat] = c0 + cs
+
+
+def step_edges(x_ref, up_ref, dn_ref, fc_ref, k_ref, has_up, has_dn):
+    fields, layers, width, members, lanes = x_ref.shape
+    per = layers * width
     for l in range(layers):
-        for r in range(width):
-            layer_row(l, r)
+        for r, halo, has, sign in ((0, up_ref, has_up, -1.0), (width - 1, dn_ref, has_dn, 1.0)):
+            here = (k_ref[l, r], x_ref[1, l, r], x_ref[2, l, r])
+            there = (jnp.exp(halo[0, l]) * has, halo[1, l], halo[2, l])
+            fh, fs = face(here, there, False) if sign > 0 else face(there, here, False)
+            flat = l * width + r
+            fc_ref[per + flat] = fc_ref[per + flat] + (sign * head_rate) * fh
+            fc_ref[2 * per + flat] = fc_ref[2 * per + flat] + sign * fs
+
+
+def observe(fc_ref, row_ref, col_ref, pred_ref, per):
+    groups = row_ref.shape[0]
+    members, lanes = fc_ref.shape[1:]
     rows = [jnp.broadcast_to(row_ref[g], (members, lanes)) for g in range(groups)]
     cols = [jnp.broadcast_to(col_ref[g], (members, lanes)) for g in range(groups)]
-    per = layers * width
     step = 8
     for g0 in range(0, groups, step):
         part = range(g0, min(g0 + step, groups))
@@ -106,9 +106,9 @@
 
 
 def analysis_kernel(
-    fc_ref, pred_ref, noise_ref, obs_ref, scale_ref, out_ref,
-    pbuf, nbuf, part, rsbuf, gc, gbuf, obuf, sref, cref,
-    s_pred, r_pred, s_noise, r_noise, s_fwd, r_fwd, s_rs, r_rs, s_ag, r_ag, s_back, r_back, s_loc,
+    x_ref, row_ref, col_ref, noise_ref, obs_ref, var_ref, out_ref,
+    fc_ref, pred_ref, k_ref, lay_ref, up_ref, dn_ref, pbuf, nbuf, part, rsbuf, gc, gbuf, obuf, sref, cref,
+    s_pred, r_pred, s_noise, r_noise, s_fwd, r_fwd, s_rs, r_rs, s_ag, r_ag, s_back, r_back, s_loc, s_up, r_up, s_dn, r_dn,
 ):
     nm, nt = lax.axis_size("mem"), lax.axis_size("tile")
     n = nm * nt
@@ -140,7 +140,44 @@
         return 0
 
     lax.fori_loop(1, n, greet, 0)
+    step_inside(x_ref, fc_ref, k_ref, lay_ref)
     pl.semaphore_wait(barrier, n - 1)
+
+    fields, layers, width = x_ref.shape[:3]
+    per = layers * width
+    to_up = remote(x_ref.at[:, :, 0], dn_ref, s_up, r_up, d, jnp.maximum(t - 1, 0))
+    to_dn = remote(x_ref.at[:, :, width - 1], up_ref, s_dn, r_dn, d, jnp.minimum(t + 1, nt - 1))
+
+    @pl.when(t > 0)
+    def _():
+        to_up.start()
+
+    @pl.when(t < nt - 1)
+    def _():
+        to_dn.start()
+
+    @pl.when(t > 0)
+    def _():
+        to_dn.wait_recv()
+
+    @pl.when(t == 0)
+    def _():
+        up_ref[...] = jnp.zeros_like(up_ref)
+
+    @pl.when(t < nt - 1)
+    def _():
+        to_up.wait_recv()
+
+    @pl.when(t == nt - 1)
+    def _():
+        dn_ref[...] = jnp.zeros_like(dn_ref)
+
+    step_edges(
+        x_ref, up_ref, dn_ref, fc_ref, k_ref,
+        jnp.where(t > 0, 1.0, 0.0).astype(jnp.float32),
+        jnp.where(t < nt - 1, 1.0, 0.0).astype(jnp.float32),
+    )
+    observe(fc_ref, row_ref, col_ref, pred_ref, per)
 
     for k in range(nm):
         c = lax.rem(d + k, nm)
@@ -168,11 +205,17 @@
             nbuf[d] = noise_ref[pl.ds(j * gpc, gpc)]
 
     mine = pl.ds(pl.multiple_of(d * members, members), members)
-    for k in range(1, nm):
-        c = lax.rem(d + k, nm)
-        remote(
-            fc_ref.at[pl.ds(c * crows, crows)], gbuf.at[:, mine, :], s_fwd, r_fwd, c, t
-        ).start()
+
+    def forward(first, count):
+        for k in range(1, nm):
+            c = lax.rem(d + k, nm)
+            remote(
+                fc_ref.at[pl.ds(c * crows + first, count)],
+                gbuf.at[pl.ds(first, count), mine, :], s_fwd, r_fwd, c, t,
+            ).start()
+
+    early = crows // 3
+    forward(0, early)
     local = pltpu.make_async_copy(
         fc_ref.at[pl.ds(d * crows, crows)], gbuf.at[:, mine, :], s_loc
     )
@@ -191,7 +234,7 @@
                 pred = pred + pbuf[q, :, g]
             pred = pred.reshape(total, lanes)
             noise = nbuf[:, g].reshape(total, lanes)
-            scale = scale_ref[base + g]
+            scale = jnp.sqrt(alpha_mda * var_ref[base + g])
             innov = (obs_ref[base + g] - pred) / scale + noise
             anom = (pred - jnp.mean(pred, axis=0, keepdims=True)) / (
                 scale * math.sqrt(total - 1)
@@ -241,6 +284,11 @@
             return 0
 
         lax.fori_loop(1, n, spread, 0)
+
+    forward(early, crows - early)
+
+    @pl.when(me < reducers)
+    def _():
         drain(gc.at[pl.ds(0, reducers - 1)], r_ag)
 
     if reducers < n:
@@ -267,15 +315,21 @@
         piv = pltpu.roll(rows, lax.rem(total - first, total), 1)
         own = (blane >= first) & (blane < first + b)
         z_s = jnp.where(own, jnp.where(blane == brow + first, -1.0, 0.0), rows)
-        for k in range(b):
-            inv = 1.0 / piv[k : k + 1, k : k + 1]
-            col = piv[:, k : k + 1]
-            fac = jnp.where(brow == k, 0.0, col)
-            at = brow == k
+        for k in range(0, b, 2):
+            c0 = jnp.broadcast_to(piv[:, k : k + 1], (b, total))
+            c1 = jnp.broadcast_to(piv[:, k + 1 : k + 2], (b, total))
+            p00, p10 = c0[k : k + 1], c0[k + 1 : k + 2]
+            p01, p11 = c1[k : k + 1], c1[k + 1 : k + 2]
+            inv = 1.0 / (p00 * p11 - p01 * p10)
+            pair = (brow == k) | (brow == k + 1)
+            f0, f1 = jnp.where(pair, 0.0, c0), jnp.where(pair, 0.0, c1)
 
             def upd(z):
-                new = z[k : k + 1, :] * inv
-                return jnp.where(at, new, z - fac * new)
+                z0, z1 = z[k : k + 1] * inv, z[k + 1 : k + 2] * inv
+                n0 = p11 * z0 - p01 * z1
+                n1 = p00 * z1 - p10 * z0
+                rest = z - f0 * n0 - f1 * n1
+                return jnp.where(brow == k, n0, jnp.where(brow == k + 1, n1, rest))
 
             piv, z_s, z_c = upd(piv), upd(z_s), upd(z_c)
         left = rows.T
@@ -310,6 +364,14 @@
             ).start()
     out_ref[pl.ds(d * crows, crows)] = obuf[:, mine, :]
 
+    @pl.when(t > 0)
+    def _():
+        to_up.wait_send()
+
+    @pl.when(t < nt - 1)
+    def _():
+        to_dn.wait_send()
+
     @pl.when(worker)
     def _():
         drain(pred_ref.at[pl.ds(0, (nm - 1) * gpc)], s_pred)
@@ -363,8 +425,6 @@
     nt, nm = lax.axis_size("tile"), lax.axis_size("mem")
     n = nt * nm
     x = fields_in.transpose(1, 2, 3, 0, 4)
-    up = lax.ppermute(x[:, :, width - 1], "tile", [(i, i + 1) for i in range(nt - 1)])
-    dn = lax.ppermute(x[:, :, 0], "tile", [(i + 1, i) for i in range(nt - 1)])
     plane = width * nt * lanes
     lay = offsets // plane
     rest = offsets % plane
@@ -375,21 +435,11 @@
     col = (rest % lanes).reshape(groups, 1, lanes)
     rows = fields * layers * width
     f32 = jnp.float32
-    fc, pred = pl.pallas_call(
-        forecast_kernel,
-        out_shape=(
-            jax.ShapeDtypeStruct((rows, members, lanes), f32),
-            jax.ShapeDtypeStruct((groups, members, lanes), f32),
-        ),
-        in_specs=[VM] * 5,
-        out_specs=(VM, VM),
-        scratch_shapes=[pltpu.VMEM((layers, width + 2, members, lanes), f32)],
-    )(x, up, dn, row, col)
     gpc = groups // nm
     own = groups // nt
     noise = obs_noise.reshape(own, lanes, members).transpose(0, 2, 1)
     obs = observed.reshape(own, 1, lanes)
-    scale = jnp.sqrt(alpha_mda * obs_var).reshape(own, 1, lanes)
+    var = obs_var.reshape(own, 1, lanes)
     total = members * nm
     reducers = min(n, 2 * total // 8)
     blk = 2 * total // reducers
@@ -398,9 +448,15 @@
     out = pl.pallas_call(
         analysis_kernel,
         out_shape=jax.ShapeDtypeStruct((rows, members, lanes), f32),
-        in_specs=[VM] * 5,
+        in_specs=[VM] * 6,
         out_specs=VM,
         scratch_shapes=[
+            pltpu.VMEM((rows, members, lanes), f32),
+            pltpu.VMEM((groups, members, lanes), f32),
+            pltpu.VMEM((layers, width, members, lanes), f32),
+            pltpu.VMEM((2, width, members, lanes), f32),
+            pltpu.VMEM((fields, layers, members, lanes), f32),
+            pltpu.VMEM((fields, layers, members, lanes), f32),
             pltpu.VMEM((nt, nm, gpc, members, lanes), f32),
             pltpu.VMEM((nm, gpc, members, lanes), f32),
             pltpu.VMEM((reducers, blk, total), f32),
@@ -411,9 +467,9 @@
             pltpu.VMEM((total, total), f32),
             pltpu.VMEM((total, total), f32),
         ]
-        + [dma] * 13,
+        + [dma] * 17,
         compiler_params=pltpu.CompilerParams(collective_id=0, has_side_effects=True),
-    )(fc, pred, noise, obs, scale)
+    )(x, row, col, noise, obs, var)
     return out.reshape(fields, layers, width, members, lanes).transpose(3, 0, 1, 2, 4)
 
 

time: 90.8 us -> 68.7 us (0.76)
  Pallas kernels: 78.2 us -> 61.7 us
  starting transfers between devices: 3.69 us -> 0 us
    pallas_call x1 -> x0, Pallas kernels: 9.53 us -> none  [local(): pl.pallas_call(forecast_kernel, out_shape=(jax.ShapeDtypeStruct((rows, me...]
    pallas_call x1, Pallas kernels: 68.6 us -> 61.7 us  [local(): pl.pallas_call(analysis_kernel, out_shape=jax.ShapeDtypeStruct((rows, mem...]
    ppermute x2 -> x0, starting transfers between devices: 3.69 us -> none  [the longest x1 2.4 us: local(): lax.ppermute(x[:, :, width - 1], 'tile', [(i, i + 1) for i in range(nt -...]
    transpose x1 -> x0, local copies, waits for them, and re-layouts: 1.34 us -> none  [local(): x = fields_in.transpose(1, 2, 3, 0, 4)]
    unnamed x13 -> x5, local copies, waits for them, and re-layouts: 2.46 us -> 3.17 us
  transfers between devices with their start and end apart: 2 -> 0, of which waited for: 1 -> 0; matrix products, arithmetic and copies ran while one was open for 3% -> 0% of each run, Pallas kernels for 0% -> 0%
where the time goes in v2:
time: 68.7 us; the launch traced here: 68.4 us
  Pallas kernels  61.7 us (90%)
  local copies, waits for them, and re-layouts  6.04 us (9%)
    pallas_call x1, Pallas kernels, local(): pl.pallas_call(analysis_kernel, out_shape=jax.ShapeDtypeStruct((rows, mem...  61.7 us
    unnamed x5, local copies, waits for them, and re-layouts  3.17 us
    reshape x1, local copies, waits for them, and re-layouts, local(): out.reshape(fields, layers, width, members, lanes).transpose(3, 0, 1, 2, 4)  2.27 us

profile of v2, /device:TPU:0, one launch (start us, length us, event | category | flops | bytes accessed | tf_op | source)
XLA Modules:
  0.0 68.4 jit_solution(12304568998274419881)
XLA Ops:
  0.0 0.0 copy-start
  0.0 0.0 copy-start.1
  0.0 0.7 %copy-done.1 = s32[1024]{0:T(1024)S(1)} copy-done((s32[1024]{0:T(1024)S(1)}, s32[1024]{0:T(1024)}, u32[]{:S(2)}) %copy-start.1) | copy-done | bytes 4120
  0.7 0.6 add_select_fusion
  1.3 0.0 copy-done
  1.3 0.6 bitcast_bitcast_fusion.noise_ref
  1.9 2.5 %copy.16 = f32[16,3,4,8,128]{4,0,3,2,1:T(8,128)} copy(f32[16,3,4,8,128]{4,3,2,1,0:T(8,128)} %param.5) | data formatting | bytes 1572864 | tf_op args[0]
  4.4 61.7 %shard_map.55 = f32[96,16,128]{2,1,0:T(8,128)} custom-call(f32[3,4,8,16,128]{4,3,2,1,0:T(8,128)} %bitcast.19, s32[8,1,128]{2,1,0:T(1,128)} %bitcast.21, s32[8,1,128]{2,1,0:T(1,128)} %bitcast.20, f32[2,16,128]{2,1,0:T(8,128)} %bitcast_bitcast_fusion.noise_ref, f32[2,1,128]{2,1,0:T(1,128)} %bitcast.22, f32[2,1,128]{2,1,0:T(1,128)} %bitcast.23), custom_call_target="tpu_custom_call" | custom-call | tf_op jit(solution)/shard_map/pallas_call | solution.py:448
  66.1 2.3 %copy.15 = f32[3,4,8,16,128]{4,2,1,0,3:T(8,128)} copy(f32[3,4,8,16,128]{4,3,2,1,0:T(8,128)} %bitcast.18) | data formatting | bytes 1572864 | tf_op jit(solution)/shard_map/reshape | solution.py:473
Async XLA Ops:
  0.0 1.3 %copy-start = (f32[256,16]{0,1:T(8,128)S(1)}, f32[256,16]{0,1:T(8,128)}, u32[]{:S(2)}) copy-start(f32[256,16]{0,1:T(8,128)} %param.9) | copy-start | bytes 49156
  0.0 0.7 %copy-start.1 = (s32[1024]{0:T(1024)S(1)}, s32[1024]{0:T(1024)}, u32[]{:S(2)}) copy-start(s32[1024]{0:T(1024)} %param.6) | copy-start | bytes 12292

commit v3 on v2

--- a/solution.py
+++ b/solution.py
@@ -16,6 +16,16 @@
 HI = lax.Precision.HIGHEST
 MESH = pl.DeviceIdType.MESH
 VM = pl.BlockSpec(memory_space=pltpu.VMEM)
+
+
+def put(ref, flat, value):
+    count = ref.shape[1]
+    ref[flat // count, flat % count] = value
+
+
+def get(ref, flat):
+    count = ref.shape[1]
+    return ref[flat // count, flat % count]
 
 
 def face(a, b, buoyant):
@@ -64,9 +74,8 @@
                 lay_ref[1, r] = fs
                 hs, cs = hs + fh, cs + fs
             flat = l * width + r
-            fc_ref[flat] = x_ref[0, l, r]
-            fc_ref[per + flat] = h0 + head_rate * hs
-            fc_ref[2 * per + flat] = c0 + cs
+            put(fc_ref, per + flat, h0 + head_rate * hs)
+            put(fc_ref, 2 * per + flat, c0 + cs)
 
 
 def step_edges(x_ref, up_ref, dn_ref, fc_ref, k_ref, has_up, has_dn):
@@ -78,36 +87,41 @@
             there = (jnp.exp(halo[0, l]) * has, halo[1, l], halo[2, l])
             fh, fs = face(here, there, False) if sign > 0 else face(there, here, False)
             flat = l * width + r
-            fc_ref[per + flat] = fc_ref[per + flat] + (sign * head_rate) * fh
-            fc_ref[2 * per + flat] = fc_ref[2 * per + flat] + sign * fs
-
-
-def observe(fc_ref, row_ref, col_ref, pred_ref, per):
+            put(fc_ref, per + flat, get(fc_ref, per + flat) + (sign * head_rate) * fh)
+            put(fc_ref, 2 * per + flat, get(fc_ref, 2 * per + flat) + sign * fs)
+
+
+def observe(fc_ref, row_ref, hot_ref, pred_ref, per):
     groups = row_ref.shape[0]
-    members, lanes = fc_ref.shape[1:]
+    nm, members, lanes = fc_ref.shape[1:]
+    first = per // nm
     rows = [jnp.broadcast_to(row_ref[g], (members, lanes)) for g in range(groups)]
-    cols = [jnp.broadcast_to(col_ref[g], (members, lanes)) for g in range(groups)]
-    step = 8
-    for g0 in range(0, groups, step):
-        part = range(g0, min(g0 + step, groups))
-
-        def body(r, accs):
-            v = fc_ref[per + r]
-            return tuple(
-                jnp.where(rows[g] == r, jnp.take_along_axis(v, cols[g], axis=1), a)
-                for g, a in zip(part, accs)
+    for g0 in range(0, groups, 8):
+        part = range(g0, min(g0 + 8, groups))
+        hot = hot_ref[:, g0 * lanes : (part[-1] + 1) * lanes]
+        acc = [jnp.zeros((members, lanes), jnp.float32) for _ in part]
+        for j in range(2 * per // nm):
+            v = fc_ref[first + j].reshape(nm * members, lanes)
+            hi = v.astype(jnp.bfloat16)
+            left = v - hi.astype(jnp.float32)
+            mid = left.astype(jnp.bfloat16)
+            low = (left - mid.astype(jnp.float32)).astype(jnp.bfloat16)
+            picked = jnp.dot(
+                jnp.concatenate([hi, mid, low], axis=1), hot, preferred_element_type=jnp.float32
             )
-
-        accs = lax.fori_loop(
-            0, 2 * per, body, tuple(jnp.zeros((members, lanes), jnp.float32) for _ in part)
-        )
-        for g, a in zip(part, accs):
-            pred_ref[g] = a
+            for q in range(nm):
+                block = picked[q * members : (q + 1) * members]
+                for i, g in enumerate(part):
+                    acc[i] = jnp.where(
+                        rows[g] == j * nm + q, block[:, i * lanes : (i + 1) * lanes], acc[i]
+                    )
+        for i, g in enumerate(part):
+            pred_ref[g] = acc[i]
 
 
 def analysis_kernel(
-    x_ref, row_ref, col_ref, noise_ref, obs_ref, var_ref, out_ref,
-    fc_ref, pred_ref, k_ref, lay_ref, up_ref, dn_ref, pbuf, nbuf, part, rsbuf, gc, gbuf, obuf, sref, cref,
+    x_in, row_ref, col_ref, noise_in, obs_ref, var_ref, out_ref,
+    x_ref, noise_ref, hot_ref, orow, fc_ref, pred_ref, k_ref, lay_ref, up_ref, dn_ref, pbuf, nbuf, part, rsbuf, gc, gbuf, obuf, sref, cref,
     s_pred, r_pred, s_noise, r_noise, s_fwd, r_fwd, s_rs, r_rs, s_ag, r_ag, s_back, r_back, s_loc, s_up, r_up, s_dn, r_dn,
 ):
     nm, nt = lax.axis_size("mem"), lax.axis_size("tile")
@@ -140,11 +154,27 @@
         return 0
 
     lax.fori_loop(1, n, greet, 0)
+    fields, layers, width = x_ref.shape[:3]
+    per = layers * width
+    rows_all = fields * per
+    for f in range(fields):
+        for l in range(layers):
+            for r in range(width):
+                flat = f * per + l * width + r
+                value = x_in[pl.ds(flat, members, stride=rows_all), :]
+                x_ref[f, l, r] = value
+                if f == 0:
+                    put(fc_ref, flat, value)
+    for g in range(noise_ref.shape[0]):
+        noise_ref[g] = noise_in[pl.ds(g * lanes, lanes), :].T
+    lane_of = lax.broadcasted_iota(jnp.int32, (lanes, lanes), 0)
+    for g in range(col_ref.shape[0]):
+        hot = jnp.where(lane_of == col_ref[g], 1.0, 0.0).astype(jnp.bfloat16)
+        for piece in range(3):
+            hot_ref[pl.ds(piece * lanes, lanes), pl.ds(g * lanes, lanes)] = hot
     step_inside(x_ref, fc_ref, k_ref, lay_ref)
     pl.semaphore_wait(barrier, n - 1)
 
-    fields, layers, width = x_ref.shape[:3]
-    per = layers * width
     to_up = remote(x_ref.at[:, :, 0], dn_ref, s_up, r_up, d, jnp.maximum(t - 1, 0))
     to_dn = remote(x_ref.at[:, :, width - 1], up_ref, s_dn, r_dn, d, jnp.minimum(t + 1, nt - 1))
 
@@ -155,6 +185,19 @@
     @pl.when(t < nt - 1)
     def _():
         to_dn.start()
+
+    mine = pl.ds(pl.multiple_of(d * members, members), members)
+
+    def forward(first, end):
+        for k in range(1, nm):
+            c = lax.rem(d + k, nm)
+            span = pl.ds(first, end - first)
+            remote(fc_ref.at[span, c], gbuf.at[span, mine, :], s_fwd, r_fwd, c, t).start()
+
+    stage_a = per // nm
+    stage_b = stage_a + max(1, crows // 6)
+    stage_c = stage_b + max(1, crows // 3)
+    forward(0, stage_a)
 
     @pl.when(t > 0)
     def _():
@@ -177,7 +220,8 @@
         jnp.where(t > 0, 1.0, 0.0).astype(jnp.float32),
         jnp.where(t < nt - 1, 1.0, 0.0).astype(jnp.float32),
     )
-    observe(fc_ref, row_ref, col_ref, pred_ref, per)
+    forward(stage_a, stage_b)
+    observe(fc_ref, row_ref, hot_ref, pred_ref, per)
 
     for k in range(nm):
         c = lax.rem(d + k, nm)
@@ -204,22 +248,7 @@
         def _():
             nbuf[d] = noise_ref[pl.ds(j * gpc, gpc)]
 
-    mine = pl.ds(pl.multiple_of(d * members, members), members)
-
-    def forward(first, count):
-        for k in range(1, nm):
-            c = lax.rem(d + k, nm)
-            remote(
-                fc_ref.at[pl.ds(c * crows + first, count)],
-                gbuf.at[pl.ds(first, count), mine, :], s_fwd, r_fwd, c, t,
-            ).start()
-
-    early = crows // 3
-    forward(0, early)
-    local = pltpu.make_async_copy(
-        fc_ref.at[pl.ds(d * crows, crows)], gbuf.at[:, mine, :], s_loc
-    )
-    local.start()
+    forward(stage_b, stage_c)
 
     @pl.when(worker)
     def _():
@@ -285,7 +314,9 @@
 
         lax.fori_loop(1, n, spread, 0)
 
-    forward(early, crows - early)
+    forward(stage_c, crows)
+    local = pltpu.make_async_copy(fc_ref.at[:, d], gbuf.at[:, mine, :], s_loc)
+    local.start()
 
     @pl.when(me < reducers)
     def _():
@@ -349,7 +380,7 @@
 
     local.wait()
     drain(gbuf.at[:, pl.ds(0, (nm - 1) * members), :], r_fwd)
-    parts = 3 if crows % 3 == 0 else 1
+    parts = 6 if crows % 6 == 0 else 1
     pr = crows // parts
     for q in range(parts):
         for r in range(q * pr, (q + 1) * pr):
@@ -359,10 +390,10 @@
             theirs = pl.ds(pl.multiple_of(c * members, members), members)
             remote(
                 obuf.at[pl.ds(q * pr, pr), theirs, :],
-                out_ref.at[pl.ds(d * crows + q * pr, pr)],
+                orow.at[pl.ds(q * pr, pr), d],
                 s_back, r_back, c, t,
             ).start()
-    out_ref[pl.ds(d * crows, crows)] = obuf[:, mine, :]
+    orow[:, d] = obuf[:, mine, :]
 
     @pl.when(t > 0)
     def _():
@@ -409,9 +440,11 @@
             drain(gc.at[pl.ds(0, n - 1)], s_ag)
         else:
             lax.fori_loop(1, n, done, 0)
-    drain(fc_ref.at[pl.ds(0, (nm - 1) * crows)], s_fwd)
+    drain(fc_ref.at[:, pl.ds(0, nm - 1)], s_fwd)
     drain(obuf.at[:, pl.ds(0, (nm - 1) * members), :], s_back)
-    drain(out_ref.at[pl.ds(0, (nm - 1) * crows)], r_back)
+    drain(orow.at[:, pl.ds(0, nm - 1)], r_back)
+    for flat in range(rows_all):
+        out_ref[pl.ds(flat, members, stride=rows_all), :] = get(orow, flat)
 
 
 def pbuf_flat(ref, count):
@@ -424,7 +457,8 @@
     rank = lax.axis_index("tile")
     nt, nm = lax.axis_size("tile"), lax.axis_size("mem")
     n = nt * nm
-    x = fields_in.transpose(1, 2, 3, 0, 4)
+    rows = fields * layers * width
+    x = fields_in.reshape(members * rows, lanes)
     plane = width * nt * lanes
     lay = offsets // plane
     rest = offsets % plane
@@ -433,11 +467,9 @@
     groups = offsets.shape[0] // lanes
     row = row.reshape(groups, 1, lanes)
     col = (rest % lanes).reshape(groups, 1, lanes)
-    rows = fields * layers * width
     f32 = jnp.float32
     gpc = groups // nm
     own = groups // nt
-    noise = obs_noise.reshape(own, lanes, members).transpose(0, 2, 1)
     obs = observed.reshape(own, 1, lanes)
     var = obs_var.reshape(own, 1, lanes)
     total = members * nm
@@ -447,11 +479,15 @@
     dma = pltpu.SemaphoreType.DMA
     out = pl.pallas_call(
         analysis_kernel,
-        out_shape=jax.ShapeDtypeStruct((rows, members, lanes), f32),
+        out_shape=jax.ShapeDtypeStruct((members * rows, lanes), f32),
         in_specs=[VM] * 6,
         out_specs=VM,
         scratch_shapes=[
-            pltpu.VMEM((rows, members, lanes), f32),
+            pltpu.VMEM((fields, layers, width, members, lanes), f32),
+            pltpu.VMEM((own, members, lanes), f32),
+            pltpu.VMEM((3 * lanes, groups * lanes), jnp.bfloat16),
+            pltpu.VMEM((crows, nm, members, lanes), f32),
+            pltpu.VMEM((crows, nm, members, lanes), f32),
             pltpu.VMEM((groups, members, lanes), f32),
             pltpu.VMEM((layers, width, members, lanes), f32),
             pltpu.VMEM((2, width, members, lanes), f32),
@@ -469,8 +505,8 @@
         ]
         + [dma] * 17,
         compiler_params=pltpu.CompilerParams(collective_id=0, has_side_effects=True),
-    )(x, row, col, noise, obs, var)
-    return out.reshape(fields, layers, width, members, lanes).transpose(3, 0, 1, 2, 4)
+    )(x, row, col, obs_noise, obs, var)
+    return out.reshape(fields_in.shape)
 
 
 def solution(mesh):

time: 68.7 us -> 69.3 us (level)
  Pallas kernels: 61.7 us -> 64.9 us
  local copies, waits for them, and re-layouts: 6.04 us -> 3.51 us
    pallas_call x1, Pallas kernels: 61.7 us -> 64.9 us  [local(): pl.pallas_call(analysis_kernel, out_shape=jax.ShapeDtypeStruct((members *...]
    reshape x1 -> x0, local copies, waits for them, and re-layouts: 2.27 us -> none  [local(): out.reshape(fields, layers, width, members, lanes).transpose(3, 0, 1, 2, 4)]
    unnamed x5 -> x6, local copies, waits for them, and re-layouts: 3.17 us -> 3.51 us
where the time goes in v3:
time: 69.3 us; the launch traced here: 69 us
  Pallas kernels  64.9 us (94%)
  local copies, waits for them, and re-layouts  3.51 us (5%)
    pallas_call x1, Pallas kernels, local(): pl.pallas_call(analysis_kernel, out_shape=jax.ShapeDtypeStruct((members *...  64.9 us
    unnamed x6, local copies, waits for them, and re-layouts  3.51 us

profile of v3, /device:TPU:0, one launch (start us, length us, event | category | flops | bytes accessed | tf_op | source)
XLA Modules:
  0.0 69.0 jit_solution(14943263860358184987)
XLA Ops:
  0.0 0.0 copy-start.1
  0.0 0.0 copy-start
  0.0 0.7 copy-done.1
  0.7 0.6 add_select_fusion
  1.3 0.0 copy-done
  1.3 0.8 %copy.6.noise_in = f32[256,16]{1,0:T(8,128)} copy(f32[256,16]{0,1:T(8,128)S(1)} %copy-done) | data formatting | bytes 32768 | tf_op args[4]
  2.1 64.9 %shard_map.55 = f32[1536,128]{1,0:T(8,128)} custom-call(f32[1536,128]{1,0:T(8,128)} %bitcast.7, s32[8,1,128]{2,1,0:T(1,128)} %bitcast.9, s32[8,1,128]{2,1,0:T(1,128)} %bitcast.8, f32[256,16]{1,0:T(8,128)} %copy.6.noise_in, f32[2,1,128]{2,1,0:T(1,128)} %bitcast.10, f32[2,1,128]{2,1,0:T(1,128)} %bitcast.11), custom_call_target="tpu_custom_call" | custom-call | tf_op jit(solution)/shard_map/pallas_call | solution.py:480
  67.0 2.1 %copy.8 = f32[16,3,4,8,128]{4,3,2,1,0:T(8,128)} copy(f32[16,3,4,8,128]{4,3,2,1,0:T(8,128)} %bitcast.6) | data formatting | bytes 1572864
Async XLA Ops:
  0.0 0.7 copy-start.1
  0.0 1.3 %copy-start = (f32[256,16]{0,1:T(8,128)S(1)}, f32[256,16]{0,1:T(8,128)}, u32[]{:S(2)}) copy-start(f32[256,16]{0,1:T(8,128)} %param.9) | copy-start | bytes 49156

commit v4 on v3

--- a/solution.py
+++ b/solution.py
@@ -194,11 +194,6 @@
             span = pl.ds(first, end - first)
             remote(fc_ref.at[span, c], gbuf.at[span, mine, :], s_fwd, r_fwd, c, t).start()
 
-    stage_a = per // nm
-    stage_b = stage_a + max(1, crows // 6)
-    stage_c = stage_b + max(1, crows // 3)
-    forward(0, stage_a)
-
     @pl.when(t > 0)
     def _():
         to_dn.wait_recv()
@@ -220,7 +215,6 @@
         jnp.where(t > 0, 1.0, 0.0).astype(jnp.float32),
         jnp.where(t < nt - 1, 1.0, 0.0).astype(jnp.float32),
     )
-    forward(stage_a, stage_b)
     observe(fc_ref, row_ref, hot_ref, pred_ref, per)
 
     for k in range(nm):
@@ -248,7 +242,8 @@
         def _():
             nbuf[d] = noise_ref[pl.ds(j * gpc, gpc)]
 
-    forward(stage_b, stage_c)
+    early = max(1, crows // 4)
+    forward(0, early)
 
     @pl.when(worker)
     def _():
@@ -314,7 +309,7 @@
 
         lax.fori_loop(1, n, spread, 0)
 
-    forward(stage_c, crows)
+    forward(early, crows)
     local = pltpu.make_async_copy(fc_ref.at[:, d], gbuf.at[:, mine, :], s_loc)
     local.start()
 
@@ -380,7 +375,7 @@
 
     local.wait()
     drain(gbuf.at[:, pl.ds(0, (nm - 1) * members), :], r_fwd)
-    parts = 6 if crows % 6 == 0 else 1
+    parts = 3 if crows % 3 == 0 else 1
     pr = crows // parts
     for q in range(parts):
         for r in range(q * pr, (q + 1) * pr):

time: 69.3 us -> 61 us (0.88)
  Pallas kernels: 64.9 us -> 56 us
    pallas_call x1, Pallas kernels: 64.9 us -> 56 us  [local(): pl.pallas_call(analysis_kernel, out_shape=jax.ShapeDtypeStruct((members *...]
where the time goes in v4:
time: 61 us; the launch traced here: 60.1 us
  Pallas kernels  56 us (92%)
  local copies, waits for them, and re-layouts  3.51 us (6%)
  other arithmetic  0.61 us (1%)
    pallas_call x1, Pallas kernels, local(): pl.pallas_call(analysis_kernel, out_shape=jax.ShapeDtypeStruct((members *...  56 us
    unnamed x6, local copies, waits for them, and re-layouts  3.51 us

profile of v4, /device:TPU:0, one launch (start us, length us, event | category | flops | bytes accessed | tf_op | source)
XLA Modules:
  0.0 60.1 jit_solution(6614334864544742901)
XLA Ops:
  0.0 0.0 copy-start.1
  0.0 0.0 copy-start
  0.0 0.7 %copy-done.1 = s32[1024]{0:T(1024)S(1)} copy-done((s32[1024]{0:T(1024)S(1)}, s32[1024]{0:T(1024)}, u32[]{:S(2)}) %copy-start.1) | copy-done | bytes 4120
  0.7 0.6 %add_select_fusion = (s32[1024]{0:T(1024)}, s32[1024]{0:T(1024)}) fusion(s32[1024]{0:T(1024)S(1)} %copy-done.1, s32[]{:T(128)S(6)} %mul.6), kind=kLoop, calls=%fused_computation | loop fusion | flops 46080 | bytes 12292 | tf_op jit(solution)/shard_map/jit(remainder)/select_n | solution.py:464
  1.3 0.0 copy-done
  1.3 0.8 %copy.6.noise_in = f32[256,16]{1,0:T(8,128)} copy(f32[256,16]{0,1:T(8,128)S(1)} %copy-done) | data formatting | bytes 32768 | tf_op args[4]
  2.1 56.0 %shard_map.55 = f32[1536,128]{1,0:T(8,128)} custom-call(f32[1536,128]{1,0:T(8,128)} %bitcast.7, s32[8,1,128]{2,1,0:T(1,128)} %bitcast.9, s32[8,1,128]{2,1,0:T(1,128)} %bitcast.8, f32[256,16]{1,0:T(8,128)} %copy.6.noise_in, f32[2,1,128]{2,1,0:T(1,128)} %bitcast.10, f32[2,1,128]{2,1,0:T(1,128)} %bitcast.11), custom_call_target="tpu_custom_call" | custom-call | tf_op jit(solution)/shard_map/pallas_call | solution.py:475
  58.1 2.1 %copy.8 = f32[16,3,4,8,128]{4,3,2,1,0:T(8,128)} copy(f32[16,3,4,8,128]{4,3,2,1,0:T(8,128)} %bitcast.6) | data formatting | bytes 1572864
Async XLA Ops:
  0.0 0.7 %copy-start.1 = (s32[1024]{0:T(1024)S(1)}, s32[1024]{0:T(1024)}, u32[]{:S(2)}) copy-start(s32[1024]{0:T(1024)} %param.6) | copy-start | bytes 12292
  0.0 1.3 %copy-start = (f32[256,16]{0,1:T(8,128)S(1)}, f32[256,16]{0,1:T(8,128)}, u32[]{:S(2)}) copy-start(f32[256,16]{0,1:T(8,128)} %param.9) | copy-start | bytes 49156

commit v5 on v4

--- a/solution.py
+++ b/solution.py
@@ -121,7 +121,7 @@
 
 def analysis_kernel(
     x_in, row_ref, col_ref, noise_in, obs_ref, var_ref, out_ref,
-    x_ref, noise_ref, hot_ref, orow, fc_ref, pred_ref, k_ref, lay_ref, up_ref, dn_ref, pbuf, nbuf, part, rsbuf, gc, gbuf, obuf, sref, cref,
+    x_ref, noise_ref, hot_ref, fc_ref, pred_ref, k_ref, lay_ref, up_ref, dn_ref, pbuf, nbuf, part, rsbuf, gc, gbuf, obuf, sref, cref,
     s_pred, r_pred, s_noise, r_noise, s_fwd, r_fwd, s_rs, r_rs, s_ag, r_ag, s_back, r_back, s_loc, s_up, r_up, s_dn, r_dn,
 ):
     nm, nt = lax.axis_size("mem"), lax.axis_size("tile")
@@ -385,10 +385,10 @@
             theirs = pl.ds(pl.multiple_of(c * members, members), members)
             remote(
                 obuf.at[pl.ds(q * pr, pr), theirs, :],
-                orow.at[pl.ds(q * pr, pr), d],
+                out_ref.at[pl.ds(q * pr, pr), d],
                 s_back, r_back, c, t,
             ).start()
-    orow[:, d] = obuf[:, mine, :]
+    out_ref[:, d] = obuf[:, mine, :]
 
     @pl.when(t > 0)
     def _():
@@ -437,9 +437,7 @@
             lax.fori_loop(1, n, done, 0)
     drain(fc_ref.at[:, pl.ds(0, nm - 1)], s_fwd)
     drain(obuf.at[:, pl.ds(0, (nm - 1) * members), :], s_back)
-    drain(orow.at[:, pl.ds(0, nm - 1)], r_back)
-    for flat in range(rows_all):
-        out_ref[pl.ds(flat, members, stride=rows_all), :] = get(orow, flat)
+    drain(out_ref.at[:, pl.ds(0, nm - 1)], r_back)
 
 
 def pbuf_flat(ref, count):
@@ -474,14 +472,13 @@
     dma = pltpu.SemaphoreType.DMA
     out = pl.pallas_call(
         analysis_kernel,
-        out_shape=jax.ShapeDtypeStruct((members * rows, lanes), f32),
+        out_shape=jax.ShapeDtypeStruct((crows, nm, members, lanes), f32),
         in_specs=[VM] * 6,
         out_specs=VM,
         scratch_shapes=[
             pltpu.VMEM((fields, layers, width, members, lanes), f32),
             pltpu.VMEM((own, members, lanes), f32),
             pltpu.VMEM((3 * lanes, groups * lanes), jnp.bfloat16),
-            pltpu.VMEM((crows, nm, members, lanes), f32),
             pltpu.VMEM((crows, nm, members, lanes), f32),
             pltpu.VMEM((groups, members, lanes), f32),
             pltpu.VMEM((layers, width, members, lanes), f32),
@@ -501,7 +498,7 @@
         + [dma] * 17,
         compiler_params=pltpu.CompilerParams(collective_id=0, has_side_effects=True),
     )(x, row, col, obs_noise, obs, var)
-    return out.reshape(fields_in.shape)
+    return out.reshape(fields, layers, width, members, lanes).transpose(3, 0, 1, 2, 4)
 
 
 def solution(mesh):

time: 61 us -> 60.5 us (level)
    reshape x0 -> x1, local copies, waits for them, and re-layouts: none -> 2.27 us  [local(): out.reshape(fields, layers, width, members, lanes).transpose(3, 0, 1, 2, 4)]
    unnamed x6 -> x5, local copies, waits for them, and re-layouts: 3.51 us -> 1.44 us
    pallas_call x1, Pallas kernels: 56 us -> 55.4 us  [local(): pl.pallas_call(analysis_kernel, out_shape=jax.ShapeDtypeStruct((crows, nm...]
where the time goes in v5:
time: 60.5 us; the launch traced here: 59.7 us
  Pallas kernels  55.4 us (92%)
  local copies, waits for them, and re-layouts  3.71 us (6%)
  other arithmetic  0.61 us (1%)
    pallas_call x1, Pallas kernels, local(): pl.pallas_call(analysis_kernel, out_shape=jax.ShapeDtypeStruct((crows, nm...  55.4 us
    reshape x1, local copies, waits for them, and re-layouts, local(): out.reshape(fields, layers, width, members, lanes).transpose(3, 0, 1, 2, 4)  2.27 us
    unnamed x5, local copies, waits for them, and re-layouts  1.44 us

profile of v5, /device:TPU:0, one launch (start us, length us, event | category | flops | bytes accessed | tf_op | source)
XLA Modules:
  0.0 59.7 jit_solution(7016784537624793140)
XLA Ops:
  0.0 0.0 copy-start.1
  0.0 0.0 copy-start
  0.0 0.7 %copy-done.1 = s32[1024]{0:T(1024)S(1)} copy-done((s32[1024]{0:T(1024)S(1)}, s32[1024]{0:T(1024)}, u32[]{:S(2)}) %copy-start.1) | copy-done | bytes 4120
  0.7 0.6 %add_select_fusion = (s32[1024]{0:T(1024)}, s32[1024]{0:T(1024)}) fusion(s32[1024]{0:T(1024)S(1)} %copy-done.1, s32[]{:T(128)S(6)} %mul.6), kind=kLoop, calls=%fused_computation.1 | loop fusion | flops 46080 | bytes 12292 | tf_op jit(solution)/shard_map/jit(remainder)/select_n | solution.py:462
  1.3 0.0 copy-done
  1.3 0.8 %copy.6.noise_in = f32[256,16]{1,0:T(8,128)} copy(f32[256,16]{0,1:T(8,128)S(1)} %copy-done) | data formatting | bytes 32768 | tf_op args[4]
  2.1 55.4 %shard_map.55 = f32[12,8,16,128]{3,2,1,0:T(8,128)} custom-call(f32[1536,128]{1,0:T(8,128)} %bitcast.10, s32[8,1,128]{2,1,0:T(1,128)} %bitcast.12, s32[8,1,128]{2,1,0:T(1,128)} %bitcast.11, f32[256,16]{1,0:T(8,128)} %copy.6.noise_in, f32[2,1,128]{2,1,0:T(1,128)} %bitcast.13, f32[2,1,128]{2,1,0:T(1,128)} %bitcast.14), custom_call_target="tpu_custom_call" | custom-call | tf_op jit(solution)/shard_map/pallas_call | solution.py:473
  57.4 2.3 %copy.9 = f32[3,4,8,16,128]{4,2,1,0,3:T(8,128)} copy(f32[3,4,8,16,128]{4,3,2,1,0:T(8,128)} %bitcast.9) | data formatting | bytes 1572864 | tf_op jit(solution)/shard_map/reshape | solution.py:501
Async XLA Ops:
  0.0 0.7 %copy-start.1 = (s32[1024]{0:T(1024)S(1)}, s32[1024]{0:T(1024)}, u32[]{:S(2)}) copy-start(s32[1024]{0:T(1024)} %param.6) | copy-start | bytes 12292
  0.0 1.3 %copy-start = (f32[256,16]{0,1:T(8,128)S(1)}, f32[256,16]{0,1:T(8,128)}, u32[]{:S(2)}) copy-start(f32[256,16]{0,1:T(8,128)} %param.9) | copy-start | bytes 49156
